TPU v7x, 128 devices: a whole 4x4x4 slice. The times are simulated.
128 devices in a mesh: srow: 16 (over x, z), scol: 4 (over y_hi, core), trow: 2 (over y_lo).
Axes of the slice: x: 4, y: 4 (y_hi: 2, y_lo: 2; y = y_hi * 2 + y_lo), z: 4, core: 2. Of those that a mesh axis runs over, the one named last changes fastest.
Arguments:
- volume: bfloat16 [8, 32, 16, 128, 128], P(None, 'srow', 'scol', 'trow'), may hold values from -6 to 6
- src_weight: bfloat16 [2, 9, 8, 8], replicated, may hold values from -0.75 to 0.75
- tgt_weight: bfloat16 [2, 9, 8, 8], replicated, may hold values from -0.75 to 0.75
- bias: float32 [2, 8], replicated, may hold values from -3 to 3
Outputs:
- refined: bfloat16 [8, 32, 16, 128, 128], P(None, 'srow', 'scol', 'trow')
All inputs are finite; a program needn't handle non-finite values.
Results may differ from a plain program's by a relative error of at most 0.0036.
Values may be sent and summed in bfloat16 or wider, within the bound.
A program may use at most 64 MiB of HBM per device.

v0:
```python
import jax
import jax.numpy as jnp
from jax import lax
from jax.sharding import PartitionSpec as P


def padded(block, sides, width):
    for axis, dim in sides:
        count = lax.axis_size(axis)
        forward = [(i, i + 1) for i in range(count - 1)]
        backward = [(target, source) for source, target in forward]
        low = lax.ppermute(
            lax.slice_in_dim(block, block.shape[dim] - width, None, axis=dim), axis, forward
        )
        high = lax.ppermute(lax.slice_in_dim(block, 0, width, axis=dim), axis, backward)
        block = jnp.concatenate([low, block, high], axis=dim)
    return block


def apply_layer(src_pad, tgt_pad, w_src, w_tgt, bias_row):
    channels, rows_two, cols_two, depth, width = src_pad.shape
    row_count = rows_two - 2
    col_count = cols_two - 2
    widened = jnp.pad(tgt_pad, ((0, 0), (0, 0), (0, 0), (0, 0), (1, 1)))
    src_kernel = jnp.transpose(w_src, (1, 0, 2)).reshape(channels, 9 * channels)
    tgt_kernel = jnp.transpose(w_tgt, (1, 0, 2)).reshape(channels, 9 * channels)
    kernel = jnp.concatenate([src_kernel, tgt_kernel], axis=1)
    out_blocks = []
    for offset in range(0, depth, 8):
        extent = min(8, depth - offset)
        pieces = []
        for first in range(3):
            for second in range(3):
                pieces.append(
                    src_pad[
                        :,
                        first : first + row_count,
                        second : second + col_count,
                        offset : offset + extent,
                    ]
                )
        for first in range(3):
            for second in range(3):
                pieces.append(
                    widened[
                        :, :, :, offset + first : offset + first + extent, second : second + width
                    ]
                )
        stacked = jnp.concatenate(pieces, axis=0)
        total = jnp.einsum("om,mijkl->oijkl", kernel, stacked, preferred_element_type=jnp.float32)
        center = tgt_pad[:, :, :, 1 + offset : 1 + offset + extent].astype(jnp.float32)
        out_blocks.append(center + jnp.maximum(total + bias_row[:, None, None, None, None], 0.0))
    return jnp.concatenate(out_blocks, axis=3)


def shards(volume, src_weight, tgt_weight, bias):
    layer_count = src_weight.shape[0]
    state = volume
    for layer_id in range(layer_count):
        src_pad = padded(state, (("srow", 1), ("scol", 2)), 1)
        tgt_pad = padded(state, (("trow", 3),), 1)
        state = apply_layer(
            src_pad, tgt_pad, src_weight[layer_id], tgt_weight[layer_id], bias[layer_id]
        ).astype(jnp.bfloat16)
    return state


def solution(mesh):
    return jax.shard_map(
        shards,
        mesh=mesh,
        in_specs=(P(None, "srow", "scol", "trow", None), P(), P(), P()),
        out_specs=P(None, "srow", "scol", "trow", None),
        check_vma=False,
    )
```

profile of v0, /device:TPU:30, one launch (start us, length us, event | category | flops | bytes accessed | tf_op | source)
XLA Modules:
  0.0 111.4 jit_solution(5178828390674980783)
XLA Ops:
  0.0 1.9 %copy.42 = bf16[8,2,4,64,128]{4,0,3,2,1:T(8,128)(2,1)S(1)} copy(bf16[8,2,4,64,128]{4,3,2,1,0:T(8,128)(2,1)} %param.4) | data formatting | bytes 2097152 | tf_op args[0]
  2.0 4.0 %collective-permute-start = (bf16[8,1,4,64,128]{4,0,3,2,1:T(8,128)(2,1)S(1)}, bf16[8,1,4,64,128]{4,0,3,2,1:T(8,128)(2,1)S(1)}, u32[]{:S(2)}, u32[]{:S(2)}) collective-permute-start(bf16[8,1,4,64,128]{4,0,3,2,1:T(8,128)(2,1)S(1)} %get-tuple-element.248), channel_id=1, source_target_pairs={{0,8},{8,16},{16,24},{24,32},{32,40},{40,48},{48,56},{56,64},{64,7... | collective-permute-start | bytes 1572872 | tf_op jit(solution)/shard_map/ppermute | solution.py:12
  6.0 1.3 %collective-permute-start.4 = (bf16[8,2,4,1,128]{4,0,3,2,1:T(8,128)(2,1)S(1)}, bf16[8,2,4,1,128]{4,0,3,2,1:T(8,128)(2,1)S(1)}, u32[]{:S(2)}, u32[]{:S(2)}) collective-permute-start(bf16[8,2,4,1,128]{4,0,3,2,1:T(8,128)(2,1)S(1)} %get-tuple-element.242), channel_id=1, source_target_pairs={{0,1},{2,3},{4,5},{6,7},{8,9},{10,11},{12,13},{14,15},{16,17},{18,... | collective-permute-start | bytes 49160 | tf_op jit(solution)/shard_map/ppermute | solution.py:12
  7.3 4.5 %collective-permute-start.5 = (bf16[8,2,4,1,128]{4,0,3,2,1:T(8,128)(2,1)S(1)}, bf16[8,2,4,1,128]{4,0,3,2,1:T(8,128)(2,1)S(1)}, u32[]{:S(2)}, u32[]{:S(2)}) collective-permute-start(bf16[8,2,4,1,128]{4,0,3,2,1:T(8,128)(2,1)S(1)} %get-tuple-element.243), channel_id=1, source_target_pairs={{1,0},{3,2},{5,4},{7,6},{9,8},{11,10},{13,12},{15,14},{17,16},{19,... | collective-permute-start | bytes 49160 | tf_op jit(solution)/shard_map/ppermute | solution.py:15
  11.9 4.3 %collective-permute-start.1 = (bf16[8,1,4,64,128]{4,0,3,2,1:T(8,128)(2,1)S(1)}, bf16[8,1,4,64,128]{4,0,3,2,1:T(8,128)(2,1)S(1)}, u32[]{:S(2)}, u32[]{:S(2)}) collective-permute-start(bf16[8,1,4,64,128]{4,0,3,2,1:T(8,128)(2,1)S(1)} %get-tuple-element.247), channel_id=1, source_target_pairs={{8,0},{16,8},{24,16},{32,24},{40,32},{48,40},{56,48},{64,56},{72,6... | collective-permute-start | bytes 1572872 | tf_op jit(solution)/shard_map/ppermute | solution.py:15
  16.2 0.6 slice_bitcast_fusion.1
  16.8 0.6 slice_bitcast_fusion
  17.4 2.9 %collective-permute-done = bf16[8,1,4,64,128]{4,0,3,2,1:T(8,128)(2,1)S(1)} collective-permute-done((bf16[8,1,4,64,128]{4,0,3,2,1:T(8,128)(2,1)S(1)}, bf16[8,1,4,64,128]{4,0,3,2,1:T(8,128)(2,1)S(1)}, u32[]{:S(2)}, u32[]{:S(2)}) %collective-permute-start) | collective-permute-done | bytes 524320 | tf_op jit(solution)/shard_map/ppermute | solution.py:12
  20.4 1.1 constant_dynamic-update-slice_fusion.6
  21.5 5.2 %collective-permute-done.1 = bf16[8,1,4,64,128]{4,0,3,2,1:T(8,128)(2,1)S(1)} collective-permute-done((bf16[8,1,4,64,128]{4,0,3,2,1:T(8,128)(2,1)S(1)}, bf16[8,1,4,64,128]{4,0,3,2,1:T(8,128)(2,1)S(1)}, u32[]{:S(2)}, u32[]{:S(2)}) %collective-permute-start.1) | collective-permute-done | bytes 524320 | tf_op jit(solution)/shard_map/ppermute | solution.py:15
  27.0 1.1 %copy-done.5 = bf16[8,3,4,64,128]{4,0,3,2,1:T(8,128)(2,1)} copy-done((bf16[8,3,4,64,128]{4,0,3,2,1:T(8,128)(2,1)}, bf16[8,3,4,64,128]{4,0,3,2,1:T(8,128)(2,1)S(1)}, u32[]{:S(2)}) %copy-start.5) | copy-done | bytes 1572888
  28.1 1.0 fusion.115
  29.2 1.9 %collective-permute-start.2 = (bf16[8,4,1,64,128]{4,0,3,2,1:T(8,128)(2,1)}, bf16[8,4,1,64,128]{4,0,3,2,1:T(8,128)(2,1)}, u32[]{:S(2)}, u32[]{:S(2)}) collective-permute-start(bf16[8,4,1,64,128]{4,0,3,2,1:T(8,128)(2,1)} %get-tuple-element.146), channel_id=1, source_target_pairs={{0,2},{2,4},{4,6},{1,3},{3,5},{5,7},{8,10},{10,12},{12,14},{9,11},... | collective-permute-start | bytes 1572872 | tf_op jit(solution)/shard_map/ppermute | solution.py:12
  31.6 5.5 %collective-permute-start.3 = (bf16[8,4,1,64,128]{4,0,3,2,1:T(8,128)(2,1)}, bf16[8,4,1,64,128]{4,0,3,2,1:T(8,128)(2,1)S(1)}, u32[]{:S(2)}, u32[]{:S(2)}) collective-permute-start(bf16[8,4,1,64,128]{4,0,3,2,1:T(8,128)(2,1)} %get-tuple-element.145), channel_id=1, source_target_pairs={{2,0},{4,2},{6,4},{3,1},{5,3},{7,5},{10,8},{12,10},{14,12},{11,9},... | collective-permute-start | bytes 1572872 | tf_op jit(solution)/shard_map/ppermute | solution.py:15
  37.1 1.1 %fusion.5 = bf16[8,2,4,66,130]{4,0,3,2,1:T(8,128)(2,1)S(1)} fusion(bf16[8,2,4,1,128]{4,0,3,2,1:T(8,128)(2,1)S(1)} %collective-permute-done.5, bf16[8,2,4,64,128]{4,0,3,2,1:T(8,128)(2,1)S(1)} %copy.42, bf16[8,2,4,1,128]{4,0,3,2,1:T(8,128)(2,1)S(1)} %collective-permute-done.4), kind=kLoop, calls=%fused_computation.103 | loop fusion | flops 6589440 | bytes 2179584 | tf_op jit(solution)/shard_map/concatenate | solution.py:16
  38.2 3.3 %collective-permute-done.2 = bf16[8,4,1,64,128]{4,0,3,2,1:T(8,128)(2,1)} collective-permute-done((bf16[8,4,1,64,128]{4,0,3,2,1:T(8,128)(2,1)}, bf16[8,4,1,64,128]{4,0,3,2,1:T(8,128)(2,1)}, u32[]{:S(2)}, u32[]{:S(2)}) %collective-permute-start.2) | collective-permute-done | bytes 524320 | tf_op jit(solution)/shard_map/ppermute | solution.py:12
  41.5 0.8 constant_dynamic-update-slice_fusion.150
  42.3 1.6 %collective-permute-done.3 = bf16[8,4,1,64,128]{4,0,3,2,1:T(8,128)(2,1)S(1)} collective-permute-done((bf16[8,4,1,64,128]{4,0,3,2,1:T(8,128)(2,1)}, bf16[8,4,1,64,128]{4,0,3,2,1:T(8,128)(2,1)S(1)}, u32[]{:S(2)}, u32[]{:S(2)}) %collective-permute-start.3) | collective-permute-done | bytes 524320 | tf_op jit(solution)/shard_map/ppermute | solution.py:15
  43.9 0.8 constant_dynamic-update-slice_fusion.147
  44.8 1.1 constant_dynamic-update-slice_fusion.144
  46.2 0.9 constant_dynamic-update-slice_fusion.129
  47.6 0.8 constant_dynamic-update-slice_fusion.111
  48.7 1.0 constant_dynamic-update-slice_fusion.126
  50.2 1.0 constant_dynamic-update-slice_fusion.108
  52.4 0.6 constant_dynamic-update-slice_fusion.139
  53.8 0.6 constant_dynamic-update-slice_fusion.136
  55.2 0.6 constant_dynamic-update-slice_fusion.133
  56.3 0.5 constant_dynamic-update-slice_fusion.157
  56.8 1.2 %constant_dynamic-update-slice_fusion.156 = (bf16[8,2,4,64,128]{4,0,3,2,1:T(8,128)(2,1)S(1)}, bf16[8,2,4,8,128]{4,0,3,2,1:T(8,128)(2,1)}) fusion(bf16[8,2,4,64,128]{4,0,3,2,1:T(8,128)(2,1)S(1)} %get-tuple-element.285, f32[8]{0:T(128)S(1)} %get-tuple-element.282, bf16[144,2,4,8,128]{4,0,3,2,1:T(8,128)(2,1)S(1)} %get-tuple-element.98, ...), kind=kOutput, calls=%fused_computation.378 | convolution fusion | flops 19206656 | bytes 2757120 | tf_op jit(solution)/shard_map/om,mijkl->oijkl/dot_general | solution.py:50
  58.0 1.2 %constant_dynamic-update-slice_fusion.155 = (bf16[8,2,4,64,128]{4,0,3,2,1:T(8,128)(2,1)S(1)}, bf16[8,2,4,8,128]{4,0,3,2,1:T(8,128)(2,1)}) fusion(bf16[8,2,4,64,128]{4,0,3,2,1:T(8,128)(2,1)S(1)} %get-tuple-element.287, f32[8]{0:T(128)S(1)} %get-tuple-element.282, bf16[144,2,4,8,128]{4,0,3,2,1:T(8,128)(2,1)S(1)} %get-tuple-element.97, ...), kind=kOutput, calls=%fused_computation.377 | convolution fusion | flops 19206656 | bytes 2757120 | tf_op jit(solution)/shard_map/om,mijkl->oijkl/dot_general | solution.py:50
  59.1 1.2 %constant_dynamic-update-slice_fusion.154 = (bf16[8,2,4,64,128]{4,0,3,2,1:T(8,128)(2,1)S(1)}, bf16[8,2,4,8,128]{4,0,3,2,1:T(8,128)(2,1)}) fusion(bf16[8,2,4,64,128]{4,0,3,2,1:T(8,128)(2,1)S(1)} %get-tuple-element.289, f32[8]{0:T(128)S(1)} %get-tuple-element.282, bf16[144,2,4,8,128]{4,0,3,2,1:T(8,128)(2,1)S(1)} %get-tuple-element.96, ...), kind=kOutput, calls=%fused_computation.376 | convolution fusion | flops 19206656 | bytes 2757120 | tf_op jit(solution)/shard_map/om,mijkl->oijkl/dot_general | solution.py:50
  60.3 1.2 %constant_dynamic-update-slice_fusion.153 = (bf16[8,2,4,64,128]{4,0,3,2,1:T(8,128)(2,1)S(1)}, bf16[8,2,4,8,128]{4,0,3,2,1:T(8,128)(2,1)}) fusion(bf16[8,2,4,64,128]{4,0,3,2,1:T(8,128)(2,1)S(1)} %get-tuple-element.291, f32[8]{0:T(128)S(1)} %get-tuple-element.282, bf16[144,2,4,8,128]{4,0,3,2,1:T(8,128)(2,1)S(1)} %get-tuple-element.95, ...), kind=kOutput, calls=%fused_computation.375 | convolution fusion | flops 19206656 | bytes 2757120 | tf_op jit(solution)/shard_map/om,mijkl->oijkl/dot_general | solution.py:50
  62.0 0.5 constant_dynamic-update-slice_fusion.151
  62.6 3.6 %collective-permute-start.6 = (bf16[8,1,4,64,128]{4,0,3,2,1:T(8,128)(2,1)S(1)}, bf16[8,1,4,64,128]{4,0,3,2,1:T(8,128)(2,1)S(1)}, u32[]{:S(2)}, u32[]{:S(2)}) collective-permute-start(bf16[8,1,4,64,128]{4,0,3,2,1:T(8,128)(2,1)S(1)} %get-tuple-element.210), channel_id=1, source_target_pairs={{0,8},{8,16},{16,24},{24,32},{32,40},{40,48},{48,56},{56,64},{64,7... | collective-permute-start | bytes 1572872 | tf_op jit(solution)/shard_map/ppermute | solution.py:12
  66.2 4.8 %collective-permute-start.7 = (bf16[8,1,4,64,128]{4,0,3,2,1:T(8,128)(2,1)S(1)}, bf16[8,1,4,64,128]{4,0,3,2,1:T(8,128)(2,1)S(1)}, u32[]{:S(2)}, u32[]{:S(2)}) collective-permute-start(bf16[8,1,4,64,128]{4,0,3,2,1:T(8,128)(2,1)S(1)} %get-tuple-element.211), channel_id=1, source_target_pairs={{8,0},{16,8},{24,16},{32,24},{40,32},{48,40},{56,48},{64,56},{72,6... | collective-permute-start | bytes 1572872 | tf_op jit(solution)/shard_map/ppermute | solution.py:15
  71.0 5.2 %collective-permute-done.6 = bf16[8,1,4,64,128]{4,0,3,2,1:T(8,128)(2,1)S(1)} collective-permute-done((bf16[8,1,4,64,128]{4,0,3,2,1:T(8,128)(2,1)S(1)}, bf16[8,1,4,64,128]{4,0,3,2,1:T(8,128)(2,1)S(1)}, u32[]{:S(2)}, u32[]{:S(2)}) %collective-permute-start.6) | collective-permute-done | bytes 524320 | tf_op jit(solution)/shard_map/ppermute | solution.py:12
  76.2 1.5 %collective-permute-done.7 = bf16[8,1,4,64,128]{4,0,3,2,1:T(8,128)(2,1)S(1)} collective-permute-done((bf16[8,1,4,64,128]{4,0,3,2,1:T(8,128)(2,1)S(1)}, bf16[8,1,4,64,128]{4,0,3,2,1:T(8,128)(2,1)S(1)}, u32[]{:S(2)}, u32[]{:S(2)}) %collective-permute-start.7) | collective-permute-done | bytes 524320 | tf_op jit(solution)/shard_map/ppermute | solution.py:15
  77.7 1.1 pad_maximum_fusion.1
  78.8 4.3 %collective-permute-start.9 = (bf16[8,4,1,64,128]{4,0,3,2,1:T(8,128)(2,1)}, bf16[8,4,1,64,128]{4,0,3,2,1:T(8,128)(2,1)S(1)}, u32[]{:S(2)}, u32[]{:S(2)}) collective-permute-start(bf16[8,4,1,64,128]{4,0,3,2,1:T(8,128)(2,1)} %get-tuple-element.143), channel_id=1, source_target_pairs={{2,0},{4,2},{6,4},{3,1},{5,3},{7,5},{10,8},{12,10},{14,12},{11,9},... | collective-permute-start | bytes 1572872 | tf_op jit(solution)/shard_map/ppermute | solution.py:15
  83.1 1.9 %collective-permute-start.8 = (bf16[8,4,1,64,128]{4,0,3,2,1:T(8,128)(2,1)}, bf16[8,4,1,64,128]{4,0,3,2,1:T(8,128)(2,1)}, u32[]{:S(2)}, u32[]{:S(2)}) collective-permute-start(bf16[8,4,1,64,128]{4,0,3,2,1:T(8,128)(2,1)} %get-tuple-element.144), channel_id=1, source_target_pairs={{0,2},{2,4},{4,6},{1,3},{3,5},{5,7},{8,10},{10,12},{12,14},{9,11},... | collective-permute-start | bytes 1572872 | tf_op jit(solution)/shard_map/ppermute | solution.py:12
  85.1 1.3 %collective-permute-start.10 = (bf16[8,2,4,1,128]{4,0,3,2,1:T(8,128)(2,1)S(1)}, bf16[8,2,4,1,128]{4,0,3,2,1:T(8,128)(2,1)S(1)}, u32[]{:S(2)}, u32[]{:S(2)}) collective-permute-start(bf16[8,2,4,1,128]{4,0,3,2,1:T(8,128)(2,1)S(1)} %slice.1626), channel_id=1, source_target_pairs={{0,1},{2,3},{4,5},{6,7},{8,9},{10,11},{12,13},{14,15},{16,17},{18,... | collective-permute-start | bytes 49160 | tf_op jit(solution)/shard_map/ppermute | solution.py:12
  86.9 4.8 %collective-permute-start.11 = (bf16[8,2,4,1,128]{4,0,3,2,1:T(8,128)(2,1)S(1)}, bf16[8,2,4,1,128]{4,0,3,2,1:T(8,128)(2,1)S(1)}, u32[]{:S(2)}, u32[]{:S(2)}) collective-permute-start(bf16[8,2,4,1,128]{4,0,3,2,1:T(8,128)(2,1)S(1)} %slice.1627), channel_id=1, source_target_pairs={{1,0},{3,2},{5,4},{7,6},{9,8},{11,10},{13,12},{15,14},{17,16},{19,... | collective-permute-start | bytes 49160 | tf_op jit(solution)/shard_map/ppermute | solution.py:15
  91.7 3.9 %collective-permute-done.8 = bf16[8,4,1,64,128]{4,0,3,2,1:T(8,128)(2,1)} collective-permute-done((bf16[8,4,1,64,128]{4,0,3,2,1:T(8,128)(2,1)}, bf16[8,4,1,64,128]{4,0,3,2,1:T(8,128)(2,1)}, u32[]{:S(2)}, u32[]{:S(2)}) %collective-permute-start.8) | collective-permute-done | bytes 524320 | tf_op jit(solution)/shard_map/ppermute | solution.py:12
  95.6 1.7 %pad_maximum_fusion = (bf16[8,4,5,64,128]{4,0,3,2,1:T(8,128)(2,1)S(1)}, bf16[8,4,5,64,128]{4,0,3,2,1:T(8,128)(2,1)S(1)}) fusion(bf16[8,4,1,64,128]{4,0,3,2,1:T(8,128)(2,1)S(1)} %collective-permute-done.9, bf16[8,1,4,64,128]{4,0,3,2,1:T(8,128)(2,1)S(1)} %collective-permute-done.7, bf16[8,2,4,64,128]{4,0,3,2,1:T(8,128)(2,1)S(1)} %get-tuple-element.297, ...), kind=kLoop, calls=%fused_computation.98 | loop fusion | flops 7864320 | bytes 8388608 | tf_op jit(solution)/shard_map/concatenate | solution.py:16
  101.5 0.6 constant_dynamic-update-slice_fusion.295
  102.9 0.5 constant_dynamic-update-slice_fusion.277
  106.7 0.5 fusion.51
  110.2 1.2 %copy.78 = bf16[8,2,4,64,128]{4,3,2,1,0:T(8,128)(2,1)} copy(bf16[8,2,4,64,128]{4,0,3,2,1:T(8,128)(2,1)S(1)} %fusion.39) | data formatting | bytes 2097152 | tf_op jit(solution)/shard_map/concatenate | solution.py:53
  (135 shorter events, 17.4 us)
Async XLA Ops:
  0.0 16.2 %copy-start.11 = (bf16[2,9,8,8]{1,3,2,0:T(8,128)(2,1)S(1)}, bf16[2,9,8,8]{1,3,2,0:T(8,128)(2,1)}, u32[]{:S(2)}) copy-start(bf16[2,9,8,8]{1,3,2,0:T(8,128)(2,1)} %param.5) | copy-start | bytes 6916
  0.0 16.8 %copy-start.12 = (bf16[2,9,8,8]{1,3,2,0:T(8,128)(2,1)S(1)}, bf16[2,9,8,8]{1,3,2,0:T(8,128)(2,1)}, u32[]{:S(2)}) copy-start(bf16[2,9,8,8]{1,3,2,0:T(8,128)(2,1)} %param.6) | copy-start | bytes 6916
  1.9 18.5 %copy-start.4 = (bf16[8,2,4,64,128]{4,3,2,1,0:T(8,128)(2,1)S(1)}, bf16[8,2,4,64,128]{4,3,2,1,0:T(8,128)(2,1)}, u32[]{:S(2)}) copy-start(bf16[8,2,4,64,128]{4,3,2,1,0:T(8,128)(2,1)} %param.4) | copy-start | bytes 3145732
  2.0 18.3 %collective-permute-start = (bf16[8,1,4,64,128]{4,0,3,2,1:T(8,128)(2,1)S(1)}, bf16[8,1,4,64,128]{4,0,3,2,1:T(8,128)(2,1)S(1)}, u32[]{:S(2)}, u32[]{:S(2)}) collective-permute-start(bf16[8,1,4,64,128]{4,0,3,2,1:T(8,128)(2,1)S(1)} %get-tuple-element.248), channel_id=1, source_target_pairs={{0,8},{8,16},{16,24},{24,32},{32,40},{40,48},{48,56},{56,64},{64,7... | collective-permute-start | bytes 1572872 | tf_op jit(solution)/shard_map/ppermute | solution.py:12
  6.0 31.1 %collective-permute-start.4 = (bf16[8,2,4,1,128]{4,0,3,2,1:T(8,128)(2,1)S(1)}, bf16[8,2,4,1,128]{4,0,3,2,1:T(8,128)(2,1)S(1)}, u32[]{:S(2)}, u32[]{:S(2)}) collective-permute-start(bf16[8,2,4,1,128]{4,0,3,2,1:T(8,128)(2,1)S(1)} %get-tuple-element.242), channel_id=1, source_target_pairs={{0,1},{2,3},{4,5},{6,7},{8,9},{10,11},{12,13},{14,15},{16,17},{18,... | collective-permute-start | bytes 49160 | tf_op jit(solution)/shard_map/ppermute | solution.py:12
  7.3 29.8 %collective-permute-start.5 = (bf16[8,2,4,1,128]{4,0,3,2,1:T(8,128)(2,1)S(1)}, bf16[8,2,4,1,128]{4,0,3,2,1:T(8,128)(2,1)S(1)}, u32[]{:S(2)}, u32[]{:S(2)}) collective-permute-start(bf16[8,2,4,1,128]{4,0,3,2,1:T(8,128)(2,1)S(1)} %get-tuple-element.243), channel_id=1, source_target_pairs={{1,0},{3,2},{5,4},{7,6},{9,8},{11,10},{13,12},{15,14},{17,16},{19,... | collective-permute-start | bytes 49160 | tf_op jit(solution)/shard_map/ppermute | solution.py:15
  11.9 14.9 %collective-permute-start.1 = (bf16[8,1,4,64,128]{4,0,3,2,1:T(8,128)(2,1)S(1)}, bf16[8,1,4,64,128]{4,0,3,2,1:T(8,128)(2,1)S(1)}, u32[]{:S(2)}, u32[]{:S(2)}) collective-permute-start(bf16[8,1,4,64,128]{4,0,3,2,1:T(8,128)(2,1)S(1)} %get-tuple-element.247), channel_id=1, source_target_pairs={{8,0},{16,8},{24,16},{32,24},{40,32},{48,40},{56,48},{64,56},{72,6... | collective-permute-start | bytes 1572872 | tf_op jit(solution)/shard_map/ppermute | solution.py:15
  21.5 6.6 %copy-start.7 = (bf16[8,3,4,64,128]{4,0,3,2,1:T(8,128)(2,1)}, bf16[8,3,4,64,128]{4,0,3,2,1:T(8,128)(2,1)S(1)}, u32[]{:S(2)}) copy-start(bf16[8,3,4,64,128]{4,0,3,2,1:T(8,128)(2,1)S(1)} %get-tuple-element.246) | copy-start | bytes 4718596
  21.5 9.6 %copy-start.13 = (f32[2,8]{1,0:T(2,128)S(1)}, f32[2,8]{1,0:T(2,128)}, u32[]{:S(2)}) copy-start(f32[2,8]{1,0:T(2,128)} %param.7) | copy-start | bytes 196
  27.0 1.2 %copy-start.5 = (bf16[8,3,4,64,128]{4,0,3,2,1:T(8,128)(2,1)}, bf16[8,3,4,64,128]{4,0,3,2,1:T(8,128)(2,1)S(1)}, u32[]{:S(2)}) copy-start(bf16[8,3,4,64,128]{4,0,3,2,1:T(8,128)(2,1)S(1)} %get-tuple-element.249) | copy-start | bytes 4718596
  29.2 12.3 %collective-permute-start.2 = (bf16[8,4,1,64,128]{4,0,3,2,1:T(8,128)(2,1)}, bf16[8,4,1,64,128]{4,0,3,2,1:T(8,128)(2,1)}, u32[]{:S(2)}, u32[]{:S(2)}) collective-permute-start(bf16[8,4,1,64,128]{4,0,3,2,1:T(8,128)(2,1)} %get-tuple-element.146), channel_id=1, source_target_pairs={{0,2},{2,4},{4,6},{1,3},{3,5},{5,7},{8,10},{10,12},{12,14},{9,11},... | collective-permute-start | bytes 1572872 | tf_op jit(solution)/shard_map/ppermute | solution.py:12
  31.6 10.7 %copy-start.8 = (bf16[8,3,4,64,128]{4,0,3,2,1:T(8,128)(2,1)S(1)}, bf16[8,3,4,64,128]{4,0,3,2,1:T(8,128)(2,1)}, u32[]{:S(2)}) copy-start(bf16[8,3,4,64,128]{4,0,3,2,1:T(8,128)(2,1)} %copy-done.7) | copy-start | bytes 4718596
  31.6 12.3 %collective-permute-start.3 = (bf16[8,4,1,64,128]{4,0,3,2,1:T(8,128)(2,1)}, bf16[8,4,1,64,128]{4,0,3,2,1:T(8,128)(2,1)S(1)}, u32[]{:S(2)}, u32[]{:S(2)}) collective-permute-start(bf16[8,4,1,64,128]{4,0,3,2,1:T(8,128)(2,1)} %get-tuple-element.145), channel_id=1, source_target_pairs={{2,0},{4,2},{6,4},{3,1},{5,3},{7,5},{10,8},{12,10},{14,12},{11,9},... | collective-permute-start | bytes 1572872 | tf_op jit(solution)/shard_map/ppermute | solution.py:15
  46.1 1.4 %copy-start.6 = (bf16[8,3,4,64,128]{4,0,3,2,1:T(8,128)(2,1)S(1)}, bf16[8,3,4,64,128]{4,0,3,2,1:T(8,128)(2,1)}, u32[]{:S(2)}) copy-start(bf16[8,3,4,64,128]{4,0,3,2,1:T(8,128)(2,1)} %copy-done.5) | copy-start | bytes 4718596
  62.5 23.9 %copy-start.10 = (bf16[8,9,8]{1,2,0:T(8,128)(2,1)S(1)}, bf16[8,9,8]{1,2,0:T(8,128)(2,1)}, u32[]{:S(2)}) copy-start(bf16[8,9,8]{1,2,0:T(8,128)(2,1)} %get-tuple-element.277) | copy-start | bytes 3460
  62.5 24.1 %copy-start.9 = (bf16[8,9,8]{1,2,0:T(8,128)(2,1)S(1)}, bf16[8,9,8]{1,2,0:T(8,128)(2,1)}, u32[]{:S(2)}) copy-start(bf16[8,9,8]{1,2,0:T(8,128)(2,1)} %get-tuple-element.279) | copy-start | bytes 3460
  62.6 13.7 %collective-permute-start.6 = (bf16[8,1,4,64,128]{4,0,3,2,1:T(8,128)(2,1)S(1)}, bf16[8,1,4,64,128]{4,0,3,2,1:T(8,128)(2,1)S(1)}, u32[]{:S(2)}, u32[]{:S(2)}) collective-permute-start(bf16[8,1,4,64,128]{4,0,3,2,1:T(8,128)(2,1)S(1)} %get-tuple-element.210), channel_id=1, source_target_pairs={{0,8},{8,16},{16,24},{24,32},{32,40},{40,48},{48,56},{56,64},{64,7... | collective-permute-start | bytes 1572872 | tf_op jit(solution)/shard_map/ppermute | solution.py:12
  66.2 11.5 %collective-permute-start.7 = (bf16[8,1,4,64,128]{4,0,3,2,1:T(8,128)(2,1)S(1)}, bf16[8,1,4,64,128]{4,0,3,2,1:T(8,128)(2,1)S(1)}, u32[]{:S(2)}, u32[]{:S(2)}) collective-permute-start(bf16[8,1,4,64,128]{4,0,3,2,1:T(8,128)(2,1)S(1)} %get-tuple-element.211), channel_id=1, source_target_pairs={{8,0},{16,8},{24,16},{32,24},{40,32},{48,40},{56,48},{64,56},{72,6... | collective-permute-start | bytes 1572872 | tf_op jit(solution)/shard_map/ppermute | solution.py:15
  78.8 12.9 %collective-permute-start.9 = (bf16[8,4,1,64,128]{4,0,3,2,1:T(8,128)(2,1)}, bf16[8,4,1,64,128]{4,0,3,2,1:T(8,128)(2,1)S(1)}, u32[]{:S(2)}, u32[]{:S(2)}) collective-permute-start(bf16[8,4,1,64,128]{4,0,3,2,1:T(8,128)(2,1)} %get-tuple-element.143), channel_id=1, source_target_pairs={{2,0},{4,2},{6,4},{3,1},{5,3},{7,5},{10,8},{12,10},{14,12},{11,9},... | collective-permute-start | bytes 1572872 | tf_op jit(solution)/shard_map/ppermute | solution.py:15
  83.1 12.5 %collective-permute-start.8 = (bf16[8,4,1,64,128]{4,0,3,2,1:T(8,128)(2,1)}, bf16[8,4,1,64,128]{4,0,3,2,1:T(8,128)(2,1)}, u32[]{:S(2)}, u32[]{:S(2)}) collective-permute-start(bf16[8,4,1,64,128]{4,0,3,2,1:T(8,128)(2,1)} %get-tuple-element.144), channel_id=1, source_target_pairs={{0,2},{2,4},{4,6},{1,3},{3,5},{5,7},{8,10},{10,12},{12,14},{9,11},... | collective-permute-start | bytes 1572872 | tf_op jit(solution)/shard_map/ppermute | solution.py:12
  85.1 6.6 %collective-permute-start.10 = (bf16[8,2,4,1,128]{4,0,3,2,1:T(8,128)(2,1)S(1)}, bf16[8,2,4,1,128]{4,0,3,2,1:T(8,128)(2,1)S(1)}, u32[]{:S(2)}, u32[]{:S(2)}) collective-permute-start(bf16[8,2,4,1,128]{4,0,3,2,1:T(8,128)(2,1)S(1)} %slice.1626), channel_id=1, source_target_pairs={{0,1},{2,3},{4,5},{6,7},{8,9},{10,11},{12,13},{14,15},{16,17},{18,... | collective-permute-start | bytes 49160 | tf_op jit(solution)/shard_map/ppermute | solution.py:12
  86.9 13.7 %collective-permute-start.11 = (bf16[8,2,4,1,128]{4,0,3,2,1:T(8,128)(2,1)S(1)}, bf16[8,2,4,1,128]{4,0,3,2,1:T(8,128)(2,1)S(1)}, u32[]{:S(2)}, u32[]{:S(2)}) collective-permute-start(bf16[8,2,4,1,128]{4,0,3,2,1:T(8,128)(2,1)S(1)} %slice.1627), channel_id=1, source_target_pairs={{1,0},{3,2},{5,4},{7,6},{9,8},{11,10},{13,12},{15,14},{17,16},{19,... | collective-permute-start | bytes 49160 | tf_op jit(solution)/shard_map/ppermute | solution.py:15
  97.8 0.9 copy-start.3
  97.8 1.0 copy-start
  98.1 0.9 copy-start.1
  98.1 1.0 copy-start.2
where the time goes:
time: 112 us; the launch traced here: 111 us
  starting transfers between devices  42.2 us (38%)
  waiting for transfers between devices  23.6 us (21%)
  local copies, waits for them, and re-layouts  21.1 us (19%)
  other arithmetic  12.9 us (12%)
  matrix products  10.6 us (9%)
    ppermute x6, starting transfers between devices, padded(): lax.ppermute(lax.slice_in_dim(block, 0, width, axis=dim), axis, backward)  28.2 us
    ppermute x6, waiting for transfers between devices, padded(): lax.ppermute(lax.slice_in_dim(block, block.shape[dim] - width, None, axis...  15.3 us
    ppermute x6, starting transfers between devices, padded(): lax.ppermute(lax.slice_in_dim(block, block.shape[dim] - width, None, axis...  14 us
    unnamed x82, local copies, waits for them, and re-layouts  13.1 us
    dot_general x16, matrix products, apply_layer(): jnp.einsum('om,mijkl->oijkl', kernel, stacked, preferred_element_type=jnp...  10.6 us
    unnamed x31, other arithmetic  8.99 us
    ppermute x6, waiting for transfers between devices, padded(): lax.ppermute(lax.slice_in_dim(block, 0, width, axis=dim), axis, backward)  8.24 us
    concatenate x3, other arithmetic, padded(): block = jnp.concatenate([low, block, high], axis=dim)  3.9 us
  transfers between devices with their start and end apart: 12, of which 7 were waited for; matrix products, arithmetic and copies ran while one was open for 10% of the time, Pallas kernels for 0%

commit v1 on v0

v1 whole, which is shorter than its diff:
```python
import functools

import jax
import jax.numpy as jnp
from jax import lax
from jax.experimental import pallas as pl
from jax.experimental.pallas import tpu as pltpu
from jax.sharding import PartitionSpec as P

MESH = pl.DeviceIdType.MESH
BF16 = jnp.bfloat16
F32 = jnp.float32
STEP = 16
PAD = 8


def iota(shape, dim):
    return lax.broadcasted_iota(jnp.int32, shape, dim)


def expand(rows_of, taps):
    spread = (iota((8, 128), 1) // STEP == iota((8, 128), 0)).astype(BF16)
    wide = jnp.dot(taps, spread, preferred_element_type=F32)
    wide = jnp.concatenate([wide[8 * tap : 8 * tap + 8] for tap in range(9)], axis=1)
    return jnp.dot(rows_of, wide.astype(BF16), preferred_element_type=F32)


def build_weights(layer, ws_ref, wt_ref, src_mat, tgt_mat):
    rows = (iota((128, 8), 0) // STEP == iota((128, 8), 1)).astype(BF16)
    edge_rows = (iota((64, 8), 0) // 8 == iota((64, 8), 1)).astype(BF16)
    row, col = iota((128, 128), 0) % STEP, iota((128, 128), 1) % STEP
    zero = jnp.zeros((128, 128), F32)
    src = expand(rows, ws_ref[pl.ds(72 * layer, 72), :])
    for first in range(3):
        for second in range(3):
            tap = 3 * first + second
            block = jnp.where(row == col, src[:, 128 * tap : 128 * tap + 128], zero).astype(BF16)
            for i in range(2):
                place = 128 * (3 * (first + i) + second)
                src_mat[layer, 128 * i : 128 * i + 128, place : place + 128] = block
    for second in range(3):
        for i in range(2):
            place = 128 * (3 * (3 - 3 * i) + second)
            src_mat[layer, 128 * i : 128 * i + 128, place : place + 128] = zero.astype(BF16)
    taps = wt_ref[pl.ds(72 * layer, 72), :]
    own = expand(rows, taps)
    edge = expand(edge_rows, taps)
    edge_row, edge_col = iota((64, 128), 0) % 8, iota((64, 128), 1) % STEP
    up = (edge_row == 0) & (edge_col == STEP - 1)
    down = (edge_row == 7) & (edge_col == 0)
    for second in range(3):
        part = [slice(128 * (3 * first + second), 128 * (3 * first + second) + 128) for first in range(3)]
        block = jnp.where(col == row - 1, own[:, part[0]], zero)
        block = block + jnp.where(col == row, own[:, part[1]], zero)
        block = block + jnp.where(col == row + 1, own[:, part[2]], zero)
        place = slice(128 * second, 128 * second + 128)
        tgt_mat[layer, 0:128, place] = block.astype(BF16)
        tgt_mat[layer, 128:192, place] = jnp.where(up, edge[:, part[0]], 0.0).astype(BF16)
        tgt_mat[layer, 192:256, place] = jnp.where(down, edge[:, part[2]], 0.0).astype(BF16)


def kernel(
    sizes, x_ref, ws_ref, wt_ref, bias_ref, out_ref,
    buf0, buf1, sums0, sums1, src_mat, tgt_mat, edge_out, edge_in, staged,
    z_send, z_recv, j_send, j_recv, c_send, c_recv, e_send, e_recv, in_sem, out_sem,
):
    n_row, n_col = sizes
    channels, rows, cols, depth, width = x_ref.shape
    chunks = depth // STEP
    bufs, sums = (buf0, buf1), (sums0, sums1)
    r, s, t = lax.axis_index("srow"), lax.axis_index("scol"), lax.axis_index("trow")
    up, down = {"srow": lax.rem(r + 1, n_row)}, {"srow": lax.rem(r + n_row - 1, n_row)}
    right, left = {"scol": lax.rem(s + 1, n_col)}, {"scol": lax.rem(s + n_col - 1, n_col)}
    across = {"trow": 1 - t}
    has_up, has_down = r < n_row - 1, r > 0
    has_right, has_left = s < n_col - 1, s > 0

    def rows_of(block):
        return pl.ds(pl.multiple_of(block * STEP, STEP), STEP)

    def order(step):
        return (chunks - 1 - step) + t * (2 * step - (chunks - 1))

    def z_copy(layer, side, block):
        ks = rows_of(block)
        if layer == 0:
            src = x_ref.at[:, 0 if side == 0 else rows - 1, :, ks]
        else:
            src = buf1.at[:, 1 if side == 0 else rows, 1 : cols + 1, ks]
        return pltpu.make_async_remote_copy(
            src_ref=src,
            dst_ref=bufs[layer].at[:, rows + 1 if side == 0 else 0, 1 : cols + 1, ks],
            send_sem=z_send.at[layer, side, block],
            recv_sem=z_recv.at[layer, side, block],
            device_id=down if side == 0 else up,
            device_id_type=MESH,
        )

    def j_copy(layer, side, block):
        ks = rows_of(block)
        if layer == 0:
            src = x_ref.at[:, :, 0 if side == 0 else cols - 1, ks]
        else:
            src = buf1.at[:, 1 : rows + 1, 1 if side == 0 else cols, ks]
        return pltpu.make_async_remote_copy(
            src_ref=src,
            dst_ref=bufs[layer].at[:, 1 : rows + 1, cols + 1 if side == 0 else 0, ks],
            send_sem=j_send.at[layer, side, block],
            recv_sem=j_recv.at[layer, side, block],
            device_id=left if side == 0 else right,
            device_id_type=MESH,
        )

    def c_copy(layer, side, end, block):
        ks = rows_of(block)
        row = 0 if end == 0 else rows + 1
        return pltpu.make_async_remote_copy(
            src_ref=bufs[layer].at[:, row, 1 if side == 0 else cols, ks],
            dst_ref=bufs[layer].at[:, row, cols + 1 if side == 0 else 0, ks],
            send_sem=c_send.at[layer, side, end, block],
            recv_sem=c_recv.at[layer, side, end, block],
            device_id=left if side == 0 else right,
            device_id_type=MESH,
        )

    def e_copy(layer):
        return pltpu.make_async_remote_copy(
            src_ref=edge_out.at[layer],
            dst_ref=edge_in.at[layer],
            send_sem=e_send.at[layer],
            recv_sem=e_recv.at[layer],
            device_id=across,
            device_id_type=MESH,
        )

    z_sides = ((0, has_down, has_up), (1, has_up, has_down))
    j_sides = ((0, has_left, has_right), (1, has_right, has_left))
    ends = ((0, has_down), (1, has_up))

    barrier = pltpu.get_barrier_semaphore()
    for present, device in (
        (has_up, up), (has_down, down), (has_right, right), (has_left, left),
    ):
        @pl.when(present)
        def _():
            pl.semaphore_signal(barrier, inc=1, device_id=device, device_id_type=MESH)

    pl.semaphore_signal(barrier, inc=1, device_id=across, device_id_type=MESH)
    peers = 1 + sum(p.astype(jnp.int32) for p in (has_up, has_down, has_right, has_left))
    pl.semaphore_wait(barrier, peers)

    def send_chunk(layer, block):
        for side, sends, _ in z_sides:
            @pl.when(sends)
            def _():
                z_copy(layer, side, block).start()

        for side, sends, _ in j_sides:
            @pl.when(sends)
            def _():
                j_copy(layer, side, block).start()

    @pl.loop(0, chunks)
    def _(step):
        send_chunk(0, order(step))

    local = pltpu.make_async_copy(x_ref, buf0.at[:, 1 : rows + 1, 1 : cols + 1], in_sem)
    local.start()

    for buf in bufs:
        for row, present in ((0, has_down), (rows + 1, has_up)):
            @pl.when(jnp.logical_not(present))
            def _():
                buf[:, row] = jnp.zeros((channels, cols + 2, depth, width), BF16)

        for col, present in ((0, has_left), (cols + 1, has_right)):
            @pl.when(jnp.logical_not(present))
            def _():
                buf[:, :, col] = jnp.zeros((channels, rows + 2, depth, width), BF16)

    for layer in range(2):
        build_weights(layer, ws_ref, wt_ref, src_mat, tgt_mat)
        spare = jnp.zeros((channels, rows, cols, PAD, width), F32)
        sums[layer][:, :, :, 0:PAD] = spare
        sums[layer][:, :, :, depth + PAD : depth + 2 * PAD] = spare
        for channel in range(channels):
            sums[layer][channel, :, :, PAD : depth + PAD] = jnp.full(
                (rows, cols, depth, width), bias_ref[layer, channel], F32
            )

    lane = iota((channels * STEP, width), 1)

    def target_pass(layer, block):
        buf, total = bufs[layer], sums[layer]
        ks = rows_of(block)
        base = pl.multiple_of(block * STEP, STEP)
        for i in range(rows):
            for pair in range(cols // 2):
                shifted = [[], [], []]
                for n in range(2):
                    tile = buf[:, i + 1, 1 + 2 * pair + n, ks].reshape(channels * STEP, width)
                    wide = tile.astype(F32)
                    before = jnp.where(lane == 0, 0.0, pltpu.roll(wide, 1, 1))
                    after = jnp.where(lane == width - 1, 0.0, pltpu.roll(wide, width - 1, 1))
                    for second, piece in enumerate((before.astype(BF16), tile, after.astype(BF16))):
                        shifted[second].append(piece)
                stack = jnp.concatenate([jnp.concatenate(p, axis=1) for p in shifted], axis=0)
                got = jnp.dot(tgt_mat[layer], stack, preferred_element_type=F32)
                for n in range(2):
                    j = 2 * pair + n
                    part = got[:, width * n : width * n + width]
                    total[:, i, j, pl.ds(base + PAD, STEP)] += part[0:128].reshape(channels, STEP, width)
                    total[:, i, j, pl.ds(base + PAD + STEP, PAD)] += part[128:192].reshape(channels, PAD, width)
                    total[:, i, j, pl.ds(base, PAD)] += part[192:256].reshape(channels, PAD, width)

    def edge_start(layer):
        for half, place in ((0, depth + PAD), (1, PAD - 1)):
            @pl.when(t == half)
            def _():
                for i in range(rows):
                    for j in range(cols):
                        edge_out[layer, i, j] = sums[layer][:, i, j, place]

        e_copy(layer).start()

    def edge_add(layer):
        e_copy(layer).wait_recv()
        for half, place in ((0, depth + PAD - 1), (1, PAD)):
            @pl.when(t == half)
            def _():
                for i in range(rows):
                    for j in range(cols):
                        sums[layer][:, i, j, place] += edge_in[layer, i, j]

    def finish(layer, block):
        buf = bufs[layer]
        ks = rows_of(block)
        base = pl.multiple_of(block * STEP, STEP)
        for pair in range(cols // 2):
            tiles = [
                [buf[:, a, 2 * pair + b, ks].reshape(channels * STEP, width) for b in range(4)]
                for a in range(rows + 2)
            ]
            stack = jnp.concatenate(
                [
                    jnp.concatenate([tiles[a][b], tiles[a][b + 1]], axis=1)
                    for a in range(rows + 2)
                    for b in range(3)
                ],
                axis=0,
            )
            got = jnp.dot(src_mat[layer], stack, preferred_element_type=F32)
            for i in range(rows):
                for n in range(2):
                    j = 2 * pair + n
                    part = got[128 * i : 128 * i + 128, width * n : width * n + width]
                    part = part.reshape(channels, STEP, width)
                    part = part + sums[layer][:, i, j, pl.ds(base + PAD, STEP)]
                    center = tiles[i + 1][n + 1].reshape(channels, STEP, width).astype(F32)
                    value = (center + jnp.maximum(part, 0.0)).astype(BF16)
                    if layer == 0:
                        buf1[:, i + 1, j + 1, ks] = value
                    else:
                        staged[:, i, j, ks] = value

    def out_copy(block):
        ks = rows_of(block)
        return pltpu.make_async_copy(
            staged.at[:, :, :, ks], out_ref.at[:, :, :, ks], out_sem.at[block]
        )

    local.wait()

    @pl.loop(0, chunks)
    def _(step):
        target_pass(0, order(step))

        @pl.when(step == 0)
        def _():
            edge_start(0)

    for layer in range(2):
        @pl.loop(0, chunks + 1)
        def _(step):
            @pl.when(step < chunks)
            def _():
                block = order(step)
                for end, present in ends:
                    @pl.when(present)
                    def _():
                        z_copy(layer, 1 - end, block).wait_recv()
                        for side, sends, _ in j_sides:
                            @pl.when(sends)
                            def _():
                                c_copy(layer, side, end, block).start()

            @pl.when(step == 1)
            def _():
                edge_add(layer)

            @pl.when(step >= 1)
            def _():
                block = order(step - 1)
                for side, _, receives in j_sides:
                    @pl.when(receives)
                    def _():
                        j_copy(layer, side, block).wait_recv()

                    for end, present in ends:
                        @pl.when(receives & present)
                        def _():
                            c_copy(layer, side, end, block).wait_recv()

                finish(layer, block)
                if layer == 0:
                    send_chunk(1, block)
                    target_pass(1, block)

                    @pl.when(step == 1)
                    def _():
                        edge_start(1)
                else:
                    out_copy(block).start()

    @pl.loop(0, chunks)
    def _(block):
        for layer in range(2):
            for side, sends, _ in z_sides:
                @pl.when(sends)
                def _():
                    z_copy(layer, side, block).wait_send()

            for side, sends, _ in j_sides:
                @pl.when(sends)
                def _():
                    j_copy(layer, side, block).wait_send()

                for end, present in ends:
                    @pl.when(sends & present)
                    def _():
                        c_copy(layer, side, end, block).wait_send()

        out_copy(block).wait()

    for layer in range(2):
        e_copy(layer).wait_send()


def shards(sizes, volume, src_weight, tgt_weight, bias):
    channels, rows, cols, depth, width = volume.shape
    chunks = depth // STEP
    padded = pltpu.VMEM((channels, rows + 2, cols + 2, depth, width), BF16)
    total = pltpu.VMEM((channels, rows, cols, depth + 2 * PAD, width), F32)
    edges = pltpu.VMEM((2, rows, cols, channels, width), F32)
    dma = pltpu.SemaphoreType.DMA
    return pl.pallas_call(
        functools.partial(kernel, sizes),
        out_shape=jax.ShapeDtypeStruct(volume.shape, BF16),
        in_specs=[
            pl.BlockSpec(memory_space=pl.ANY),
            pl.BlockSpec(memory_space=pltpu.VMEM),
            pl.BlockSpec(memory_space=pltpu.VMEM),
            pl.BlockSpec(memory_space=pltpu.SMEM),
        ],
        out_specs=pl.BlockSpec(memory_space=pl.ANY),
        scratch_shapes=[
            padded, padded, total, total,
            pltpu.VMEM((2, 256, 12 * 128), BF16),
            pltpu.VMEM((2, 256, 3 * 128), BF16),
            edges, edges,
            pltpu.VMEM(volume.shape, BF16),
            dma((2, 2, chunks)), dma((2, 2, chunks)),
            dma((2, 2, chunks)), dma((2, 2, chunks)),
            dma((2, 2, 2, chunks)), dma((2, 2, 2, chunks)),
            dma((2,)), dma((2,)),
            dma, dma((chunks,)),
        ],
        compiler_params=pltpu.CompilerParams(
            collective_id=0, has_side_effects=True, vmem_limit_bytes=40 * 1024 * 1024
        ),
    )(volume, src_weight.reshape(-1, channels), tgt_weight.reshape(-1, channels), bias)


def solution(mesh):
    sizes = (mesh.shape["srow"], mesh.shape["scol"])
    return jax.shard_map(
        functools.partial(shards, sizes),
        mesh=mesh,
        in_specs=(P(None, "srow", "scol", "trow", None), P(), P(), P()),
        out_specs=P(None, "srow", "scol", "trow", None),
        check_vma=False,
    )
```

time: 112 us -> 40.7 us (0.36)
  the two profiles are of different devices: /device:TPU:30 before, /device:TPU:7 now
where the time goes in v1:
time: 40.7 us; the launch traced here: 40.5 us
  Pallas kernels  36.5 us (90%)
  local copies, waits for them, and re-layouts  4 us (10%)
    pallas_call x1, Pallas kernels, shards(): pl.pallas_call(functools.partial(kernel, sizes), out_shape=jax.ShapeDtype...  36.5 us
    unnamed x9, local copies, waits for them, and re-layouts  4 us

profile of v1, /device:TPU:7, one launch (start us, length us, event | category | flops | bytes accessed | tf_op | source)
XLA Modules:
  0.0 40.5 jit_solution(11009491435639077481)
XLA Ops:
  0.0 0.0 copy-start.2
  0.0 0.9 %copy.5 = bf16[2,9,8,8]{3,2,1,0:T(8,128)(2,1)S(1)} copy(bf16[2,9,8,8]{1,3,2,0:T(8,128)(2,1)} %param.5) | data formatting | bytes 4608 | tf_op args[1]
  0.9 0.0 copy-done.2
  0.9 0.2 copy.6
  1.1 0.0 copy-start.1
  1.1 0.7 %copy-done.1 = f32[2,8]{1,0:T(2,128)S(1)} copy-done((f32[2,8]{1,0:T(2,128)S(1)}, f32[2,8]{1,0:T(2,128)}, u32[]{:S(2)}) %copy-start.1) | copy-done | bytes 88
  1.8 0.0 copy-start
  1.8 1.2 %copy-done = bf16[8,2,4,64,128]{4,3,2,1,0:T(8,128)(2,1)S(1)} copy-done((bf16[8,2,4,64,128]{4,3,2,1,0:T(8,128)(2,1)S(1)}, bf16[8,2,4,64,128]{4,3,2,1,0:T(8,128)(2,1)}, u32[]{:S(2)}) %copy-start) | copy-done | bytes 1048600
  3.0 36.5 %shard_map.46 = bf16[8,2,4,64,128]{4,3,2,1,0:T(8,128)(2,1)S(1)} custom-call(bf16[8,2,4,64,128]{4,3,2,1,0:T(8,128)(2,1)S(1)} %copy-done, bf16[144,8]{1,0:T(8,128)(2,1)S(1)} %bitcast.2, bf16[144,8]{1,0:T(8,128)(2,1)S(1)} %bitcast.3, f32[2,8]{1,0:T(2,128)S(1)} %copy-done.1), custom_call_target="tpu_custom_call" | custom-call | tf_op jit(solution)/shard_map/pallas_call | solution.py:356
  39.5 1.0 %copy.8 = bf16[8,2,4,64,128]{4,3,2,1,0:T(8,128)(2,1)} copy(bf16[8,2,4,64,128]{4,3,2,1,0:T(8,128)(2,1)S(1)} %shard_map.46) | data formatting | bytes 2097152
Async XLA Ops:
  0.0 0.9 %copy-start.2 = (bf16[2,9,8,8]{1,3,2,0:T(8,128)(2,1)S(1)}, bf16[2,9,8,8]{1,3,2,0:T(8,128)(2,1)}, u32[]{:S(2)}) copy-start(bf16[2,9,8,8]{1,3,2,0:T(8,128)(2,1)} %param.6) | copy-start | bytes 6916
  1.1 0.7 %copy-start.1 = (f32[2,8]{1,0:T(2,128)S(1)}, f32[2,8]{1,0:T(2,128)}, u32[]{:S(2)}) copy-start(f32[2,8]{1,0:T(2,128)} %bias_ref.1) | copy-start | bytes 196
  1.8 1.2 %copy-start = (bf16[8,2,4,64,128]{4,3,2,1,0:T(8,128)(2,1)S(1)}, bf16[8,2,4,64,128]{4,3,2,1,0:T(8,128)(2,1)}, u32[]{:S(2)}) copy-start(bf16[8,2,4,64,128]{4,3,2,1,0:T(8,128)(2,1)} %x_ref.1) | copy-start | bytes 3145732

commit v2 on v1

--- a/solution.py
+++ b/solution.py
@@ -11,6 +11,7 @@
 BF16 = jnp.bfloat16
 F32 = jnp.float32
 STEP = 16
+LEAD = 2
 PAD = 8
 
 
@@ -18,19 +19,19 @@
     return lax.broadcasted_iota(jnp.int32, shape, dim)
 
 
-def expand(rows_of, taps):
-    spread = (iota((8, 128), 1) // STEP == iota((8, 128), 0)).astype(BF16)
-    wide = jnp.dot(taps, spread, preferred_element_type=F32)
-    wide = jnp.concatenate([wide[8 * tap : 8 * tap + 8] for tap in range(9)], axis=1)
-    return jnp.dot(rows_of, wide.astype(BF16), preferred_element_type=F32)
+def expand(rows, taps):
+    mine = iota((64, 128), 1) // STEP == iota((64, 128), 0) % 8
+    wide = [jnp.where(mine, jnp.broadcast_to(taps[:, tap : tap + 1], (64, 128)), 0.0) for tap in range(9)]
+    share = rows // 8
+    spread = (iota((rows, 64), 0) // share == iota((rows, 64), 1) // 8).astype(BF16)
+    wide = jnp.concatenate(wide, axis=1).astype(BF16)
+    return jnp.dot(spread, wide, preferred_element_type=F32)
 
 
 def build_weights(layer, ws_ref, wt_ref, src_mat, tgt_mat):
-    rows = (iota((128, 8), 0) // STEP == iota((128, 8), 1)).astype(BF16)
-    edge_rows = (iota((64, 8), 0) // 8 == iota((64, 8), 1)).astype(BF16)
     row, col = iota((128, 128), 0) % STEP, iota((128, 128), 1) % STEP
     zero = jnp.zeros((128, 128), F32)
-    src = expand(rows, ws_ref[pl.ds(72 * layer, 72), :])
+    src = expand(128, ws_ref[pl.ds(64 * layer, 64), :].astype(F32))
     for first in range(3):
         for second in range(3):
             tap = 3 * first + second
@@ -42,9 +43,9 @@
         for i in range(2):
             place = 128 * (3 * (3 - 3 * i) + second)
             src_mat[layer, 128 * i : 128 * i + 128, place : place + 128] = zero.astype(BF16)
-    taps = wt_ref[pl.ds(72 * layer, 72), :]
-    own = expand(rows, taps)
-    edge = expand(edge_rows, taps)
+    taps = wt_ref[pl.ds(64 * layer, 64), :].astype(F32)
+    own = expand(128, taps)
+    edge = expand(64, taps)
     edge_row, edge_col = iota((64, 128), 0) % 8, iota((64, 128), 1) % STEP
     up = (edge_row == 0) & (edge_col == STEP - 1)
     down = (edge_row == 7) & (edge_col == 0)
@@ -60,7 +61,8 @@
 
 
 def kernel(
-    sizes, x_ref, ws_ref, wt_ref, bias_ref, out_ref,
+    sizes, x_ref, ws_hbm, wt_hbm, bias_hbm, out_ref,
+    ws_ref, wt_ref, bias_ref,
     buf0, buf1, sums0, sums1, src_mat, tgt_mat, edge_out, edge_in, staged,
     z_send, z_recv, j_send, j_recv, c_send, c_recv, e_send, e_recv, in_sem, out_sem,
 ):
@@ -81,17 +83,18 @@
     def order(step):
         return (chunks - 1 - step) + t * (2 * step - (chunks - 1))
 
-    def z_copy(layer, side, block):
-        ks = rows_of(block)
+    def z_copy(layer, side, part, block):
+        ks = rows_of(block)
+        lo, hi = ((1, 2), (cols, cols + 1), (2, cols))[part]
         if layer == 0:
-            src = x_ref.at[:, 0 if side == 0 else rows - 1, :, ks]
+            src = x_ref.at[:, 0 if side == 0 else rows - 1, lo - 1 : hi - 1, ks]
         else:
-            src = buf1.at[:, 1 if side == 0 else rows, 1 : cols + 1, ks]
+            src = buf1.at[:, 1 if side == 0 else rows, lo:hi, ks]
         return pltpu.make_async_remote_copy(
             src_ref=src,
-            dst_ref=bufs[layer].at[:, rows + 1 if side == 0 else 0, 1 : cols + 1, ks],
-            send_sem=z_send.at[layer, side, block],
-            recv_sem=z_recv.at[layer, side, block],
+            dst_ref=bufs[layer].at[:, rows + 1 if side == 0 else 0, lo:hi, ks],
+            send_sem=z_send.at[layer, side, part, block],
+            recv_sem=z_recv.at[layer, side, part, block],
             device_id=down if side == 0 else up,
             device_id_type=MESH,
         )
@@ -149,22 +152,48 @@
     peers = 1 + sum(p.astype(jnp.int32) for p in (has_up, has_down, has_right, has_left))
     pl.semaphore_wait(barrier, peers)
 
-    def send_chunk(layer, block):
+    def send_outer(layer, block):
         for side, sends, _ in z_sides:
             @pl.when(sends)
             def _():
-                z_copy(layer, side, block).start()
+                z_copy(layer, side, 0, block).start()
+                z_copy(layer, side, 1, block).start()
 
         for side, sends, _ in j_sides:
             @pl.when(sends)
             def _():
                 j_copy(layer, side, block).start()
 
+    def send_inner(layer, block):
+        for side, sends, _ in z_sides:
+            @pl.when(sends)
+            def _():
+                z_copy(layer, side, 2, block).start()
+
+    def send_chunk(layer, step):
+        send_outer(layer, order(step))
+
+        @pl.when(step >= LEAD)
+        def _():
+            send_inner(layer, order(step - LEAD))
+
+        @pl.when(step == chunks - 1)
+        def _():
+            for late in range(LEAD):
+                send_inner(layer, order(chunks - LEAD + late))
+
     @pl.loop(0, chunks)
     def _(step):
-        send_chunk(0, order(step))
-
-    local = pltpu.make_async_copy(x_ref, buf0.at[:, 1 : rows + 1, 1 : cols + 1], in_sem)
+        send_chunk(0, step)
+
+    local = pltpu.make_async_copy(x_ref, buf0.at[:, 1 : rows + 1, 1 : cols + 1], in_sem.at[0])
+    small = [
+        pltpu.make_async_copy(ws_hbm, ws_ref, in_sem.at[1]),
+        pltpu.make_async_copy(wt_hbm, wt_ref, in_sem.at[2]),
+        pltpu.make_async_copy(bias_hbm, bias_ref, in_sem.at[3]),
+    ]
+    for copy in small:
+        copy.start()
     local.start()
 
     for buf in bufs:
@@ -178,6 +207,8 @@
             def _():
                 buf[:, :, col] = jnp.zeros((channels, rows + 2, depth, width), BF16)
 
+    for copy in small:
+        copy.wait()
     for layer in range(2):
         build_weights(layer, ws_ref, wt_ref, src_mat, tgt_mat)
         spare = jnp.zeros((channels, rows, cols, PAD, width), F32)
@@ -232,31 +263,39 @@
                     for j in range(cols):
                         sums[layer][:, i, j, place] += edge_in[layer, i, j]
 
-    def finish(layer, block):
+    def stack_of(layer, ks, pair, source_rows):
         buf = bufs[layer]
-        ks = rows_of(block)
+        parts = []
+        for a in source_rows:
+            tiles = [buf[:, a, 2 * pair + b, ks].reshape(channels * STEP, width) for b in range(4)]
+            parts += [jnp.concatenate([tiles[b], tiles[b + 1]], axis=1) for b in range(3)]
+        return jnp.concatenate(parts, axis=0)
+
+    def sums_at(layer, i, j, block):
         base = pl.multiple_of(block * STEP, STEP)
+        return sums[layer].at[:, i, j, pl.ds(base + PAD, STEP)]
+
+    def own_rows_pass(layer, block):
         for pair in range(cols // 2):
-            tiles = [
-                [buf[:, a, 2 * pair + b, ks].reshape(channels * STEP, width) for b in range(4)]
-                for a in range(rows + 2)
-            ]
-            stack = jnp.concatenate(
-                [
-                    jnp.concatenate([tiles[a][b], tiles[a][b + 1]], axis=1)
-                    for a in range(rows + 2)
-                    for b in range(3)
-                ],
-                axis=0,
-            )
-            got = jnp.dot(src_mat[layer], stack, preferred_element_type=F32)
+            stack = stack_of(layer, rows_of(block), pair, (1, 2))
+            got = jnp.dot(src_mat[layer, :, 384:1152], stack, preferred_element_type=F32)
             for i in range(rows):
                 for n in range(2):
+                    part = got[128 * i : 128 * i + 128, width * n : width * n + width]
+                    sums_at(layer, i, 2 * pair + n, block)[...] += part.reshape(channels, STEP, width)
+
+    def finish(layer, block):
+        ks = rows_of(block)
+        for pair in range(cols // 2):
+            for i in range(rows):
+                stack = stack_of(layer, ks, pair, (3 * i,))
+                mat = src_mat[layer, 128 * i : 128 * i + 128, 1152 * i : 1152 * i + 384]
+                got = jnp.dot(mat, stack, preferred_element_type=F32)
+                for n in range(2):
                     j = 2 * pair + n
-                    part = got[128 * i : 128 * i + 128, width * n : width * n + width]
-                    part = part.reshape(channels, STEP, width)
-                    part = part + sums[layer][:, i, j, pl.ds(base + PAD, STEP)]
-                    center = tiles[i + 1][n + 1].reshape(channels, STEP, width).astype(F32)
+                    part = got[:, width * n : width * n + width].reshape(channels, STEP, width)
+                    part = part + sums_at(layer, i, j, block)[...]
+                    center = bufs[layer][:, i + 1, j + 1, ks].astype(F32)
                     value = (center + jnp.maximum(part, 0.0)).astype(BF16)
                     if layer == 0:
                         buf1[:, i + 1, j + 1, ks] = value
@@ -279,71 +318,94 @@
         def _():
             edge_start(0)
 
+    def wait_sends():
+        @pl.loop(0, chunks)
+        def _(block):
+            for layer in range(2):
+                for side, sends, _ in z_sides:
+                    @pl.when(sends)
+                    def _():
+                        for part in range(3):
+                            z_copy(layer, side, part, block).wait_send()
+
+                for side, sends, _ in j_sides:
+                    @pl.when(sends)
+                    def _():
+                        j_copy(layer, side, block).wait_send()
+
+                    for end, present in ends:
+                        @pl.when(sends & present)
+                        def _():
+                            c_copy(layer, side, end, block).wait_send()
+
+        for layer in range(2):
+            e_copy(layer).wait_send()
+
+    lag = LEAD + 1
     for layer in range(2):
-        @pl.loop(0, chunks + 1)
+        @pl.loop(0, chunks + lag)
         def _(step):
+            @pl.when(step == lag)
+            def _():
+                edge_add(layer)
+
+            if layer == 1:
+                @pl.when(step == chunks + lag - 1)
+                def _():
+                    wait_sends()
+
+            @pl.when(step >= lag)
+            def _():
+                block = order(step - lag)
+                for side, _, receives in j_sides:
+                    for end, present in ends:
+                        @pl.when(receives & present)
+                        def _():
+                            c_copy(layer, side, end, block).wait_recv()
+
+                for end, present in ends:
+                    @pl.when(present)
+                    def _():
+                        z_copy(layer, 1 - end, 2, block).wait_recv()
+
+                finish(layer, block)
+                if layer == 0:
+                    send_chunk(1, step - lag)
+                    target_pass(1, block)
+
+                    @pl.when(step == lag)
+                    def _():
+                        edge_start(1)
+                else:
+                    out_copy(block).start()
+
             @pl.when(step < chunks)
             def _():
                 block = order(step)
                 for end, present in ends:
                     @pl.when(present)
                     def _():
-                        z_copy(layer, 1 - end, block).wait_recv()
+                        z_copy(layer, 1 - end, 0, block).wait_recv()
+                        z_copy(layer, 1 - end, 1, block).wait_recv()
                         for side, sends, _ in j_sides:
                             @pl.when(sends)
                             def _():
                                 c_copy(layer, side, end, block).start()
 
-            @pl.when(step == 1)
-            def _():
-                edge_add(layer)
-
-            @pl.when(step >= 1)
-            def _():
-                block = order(step - 1)
                 for side, _, receives in j_sides:
                     @pl.when(receives)
                     def _():
                         j_copy(layer, side, block).wait_recv()
 
-                    for end, present in ends:
-                        @pl.when(receives & present)
-                        def _():
-                            c_copy(layer, side, end, block).wait_recv()
-
-                finish(layer, block)
-                if layer == 0:
-                    send_chunk(1, block)
-                    target_pass(1, block)
-
-                    @pl.when(step == 1)
-                    def _():
-                        edge_start(1)
-                else:
-                    out_copy(block).start()
+                own_rows_pass(layer, block)
 
     @pl.loop(0, chunks)
     def _(block):
-        for layer in range(2):
-            for side, sends, _ in z_sides:
-                @pl.when(sends)
-                def _():
-                    z_copy(layer, side, block).wait_send()
-
-            for side, sends, _ in j_sides:
-                @pl.when(sends)
-                def _():
-                    j_copy(layer, side, block).wait_send()
-
-                for end, present in ends:
-                    @pl.when(sends & present)
-                    def _():
-                        c_copy(layer, side, end, block).wait_send()
-
         out_copy(block).wait()
 
-    for layer in range(2):
-        e_copy(layer).wait_send()
+
+def by_channels(weight):
+    return jnp.transpose(weight, (0, 2, 3, 1)).reshape(-1, weight.shape[1])
 
 
 def shards(sizes, volume, src_weight, tgt_weight, bias):
@@ -353,32 +415,36 @@
     total = pltpu.VMEM((channels, rows, cols, depth + 2 * PAD, width), F32)
     edges = pltpu.VMEM((2, rows, cols, channels, width), F32)
     dma = pltpu.SemaphoreType.DMA
+    operands = (volume, by_channels(src_weight), by_channels(tgt_weight), bias)
     return pl.pallas_call(
         functools.partial(kernel, sizes),
         out_shape=jax.ShapeDtypeStruct(volume.shape, BF16),
         in_specs=[
-            pl.BlockSpec(memory_space=pl.ANY),
-            pl.BlockSpec(memory_space=pltpu.VMEM),
-            pl.BlockSpec(memory_space=pltpu.VMEM),
-            pl.BlockSpec(memory_space=pltpu.SMEM),
+            pl.BlockSpec(memory_space=pltpu.HBM),
+            pl.BlockSpec(memory_space=pltpu.HBM),
+            pl.BlockSpec(memory_space=pltpu.HBM),
+            pl.BlockSpec(memory_space=pltpu.HBM),
         ],
         out_specs=pl.BlockSpec(memory_space=pl.ANY),
         scratch_shapes=[
+            pltpu.VMEM((2 * channels * channels, 9), BF16),
+            pltpu.VMEM((2 * channels * channels, 9), BF16),
+            pltpu.SMEM((2, channels), F32),
             padded, padded, total, total,
             pltpu.VMEM((2, 256, 12 * 128), BF16),
             pltpu.VMEM((2, 256, 3 * 128), BF16),
             edges, edges,
             pltpu.VMEM(volume.shape, BF16),
-            dma((2, 2, chunks)), dma((2, 2, chunks)),
+            dma((2, 2, 3, chunks)), dma((2, 2, 3, chunks)),
             dma((2, 2, chunks)), dma((2, 2, chunks)),
             dma((2, 2, 2, chunks)), dma((2, 2, 2, chunks)),
             dma((2,)), dma((2,)),
-            dma, dma((chunks,)),
+            dma((4,)), dma((chunks,)),
         ],
         compiler_params=pltpu.CompilerParams(
             collective_id=0, has_side_effects=True, vmem_limit_bytes=40 * 1024 * 1024
         ),
-    )(volume, src_weight.reshape(-1, channels), tgt_weight.reshape(-1, channels), bias)
+    )(*(pltpu.with_memory_space_constraint(v, pltpu.HBM) for v in operands))
 
 
 def solution(mesh):

time: 40.7 us -> 34.8 us (0.86)
  local copies, waits for them, and re-layouts: 4 us -> 0.97 us
  Pallas kernels: 36.5 us -> 33.7 us
    unnamed x9 -> x1, local copies, waits for them, and re-layouts: 4 us -> 0.97 us
    pallas_call x1, Pallas kernels: 36.5 us -> 33.7 us  [shards(): pl.pallas_call(functools.partial(kernel, sizes), out_shape=jax.ShapeDtype...]
where the time goes in v2:
time: 34.8 us; the launch traced here: 34.7 us
  Pallas kernels  33.7 us (97%)
  local copies, waits for them, and re-layouts  0.97 us (3%)
    pallas_call x1, Pallas kernels, shards(): pl.pallas_call(functools.partial(kernel, sizes), out_shape=jax.ShapeDtype...  33.7 us
    unnamed x1, local copies, waits for them, and re-layouts  0.97 us

profile of v2, /device:TPU:7, one launch (start us, length us, event | category | flops | bytes accessed | tf_op | source)
XLA Modules:
  0.0 34.7 jit_solution(11143101788985249168)
XLA Ops:
  0.0 33.7 %shard_map.46 = bf16[8,2,4,64,128]{4,3,2,1,0:T(8,128)(2,1)S(1)} custom-call(bf16[8,2,4,64,128]{4,3,2,1,0:T(8,128)(2,1)} %x_ref.1, bf16[128,9]{1,0:T(8,128)(2,1)} %bitcast.6, bf16[128,9]{1,0:T(8,128)(2,1)} %bitcast.7, f32[2,8]{1,0:T(2,128)} %bias_hbm.1), custom_call_target="tpu_custom_call" | custom-call | tf_op jit(solution)/shard_map/pallas_call | solution.py:419
  33.7 1.0 %copy.6 = bf16[8,2,4,64,128]{4,3,2,1,0:T(8,128)(2,1)} copy(bf16[8,2,4,64,128]{4,3,2,1,0:T(8,128)(2,1)S(1)} %shard_map.46) | data formatting | bytes 2097152

commit v3 on v2

--- a/solution.py
+++ b/solution.py
@@ -11,7 +11,8 @@
 BF16 = jnp.bfloat16
 F32 = jnp.float32
 STEP = 16
-LEAD = 2
+LEADS = (3, 3)
+Z_RING = 4
 PAD = 8
 
 
@@ -64,7 +65,7 @@
     sizes, x_ref, ws_hbm, wt_hbm, bias_hbm, out_ref,
     ws_ref, wt_ref, bias_ref,
     buf0, buf1, sums0, sums1, src_mat, tgt_mat, edge_out, edge_in, staged,
-    z_send, z_recv, j_send, j_recv, c_send, c_recv, e_send, e_recv, in_sem, out_sem,
+    z_send, z_recv, j_send, j_recv, c_send, c_recv, e_send, e_recv, in_sem, out_sem, hello,
 ):
     n_row, n_col = sizes
     channels, rows, cols, depth, width = x_ref.shape
@@ -140,51 +141,72 @@
     j_sides = ((0, has_left, has_right), (1, has_right, has_left))
     ends = ((0, has_down), (1, has_up))
 
+    first, last = lax.rem(r, Z_RING) == 0, lax.rem(r, Z_RING) == Z_RING - 1
+    up_later, down_later = has_up & jnp.logical_not(last), has_down & first
+    up_earlier, down_earlier = has_up & last, has_down & jnp.logical_not(first)
+    later = ((up_later, up), (down_later, down), (has_right, right), (t == 0, across))
+    earlier = (
+        (up_earlier, up, 1), (down_earlier, down, 0), (has_left, left, 2), (t == 1, across, 3),
+    )
     barrier = pltpu.get_barrier_semaphore()
-    for present, device in (
-        (has_up, up), (has_down, down), (has_right, right), (has_left, left),
-    ):
+    for present, device in later:
         @pl.when(present)
         def _():
             pl.semaphore_signal(barrier, inc=1, device_id=device, device_id_type=MESH)
 
-    pl.semaphore_signal(barrier, inc=1, device_id=across, device_id_type=MESH)
-    peers = 1 + sum(p.astype(jnp.int32) for p in (has_up, has_down, has_right, has_left))
-    pl.semaphore_wait(barrier, peers)
-
-    def send_outer(layer, block):
+    awaited = sum(present.astype(jnp.int32) for present, _, _ in earlier)
+
+    @pl.when(awaited > 0)
+    def _():
+        pl.semaphore_wait(barrier, awaited)
+
+    for present, device, slot in earlier:
+        @pl.when(present)
+        def _():
+            pl.semaphore_signal(hello.at[slot], inc=1, device_id=device, device_id_type=MESH)
+
+    def send_rows(layer, side, step):
+        z_copy(layer, side, 0, order(step)).start()
+        z_copy(layer, side, 1, order(step)).start()
+
+        lead = LEADS[layer]
+
+        @pl.when(step >= lead)
+        def _():
+            z_copy(layer, side, 2, order(step - lead)).start()
+
+        @pl.when(step == chunks - 1)
+        def _():
+            for late in range(lead):
+                z_copy(layer, side, 2, order(chunks - lead + late)).start()
+
+    def send_cols(layer, side, step):
+        j_copy(layer, side, order(step)).start()
+
+    def send_chunk(layer, step):
         for side, sends, _ in z_sides:
             @pl.when(sends)
             def _():
-                z_copy(layer, side, 0, block).start()
-                z_copy(layer, side, 1, block).start()
+                send_rows(layer, side, step)
 
         for side, sends, _ in j_sides:
             @pl.when(sends)
             def _():
-                j_copy(layer, side, block).start()
-
-    def send_inner(layer, block):
-        for side, sends, _ in z_sides:
-            @pl.when(sends)
-            def _():
-                z_copy(layer, side, 2, block).start()
-
-    def send_chunk(layer, step):
-        send_outer(layer, order(step))
-
-        @pl.when(step >= LEAD)
-        def _():
-            send_inner(layer, order(step - LEAD))
-
-        @pl.when(step == chunks - 1)
-        def _():
-            for late in range(LEAD):
-                send_inner(layer, order(chunks - LEAD + late))
-
-    @pl.loop(0, chunks)
-    def _(step):
-        send_chunk(0, step)
+                send_cols(layer, side, step)
+
+    def send_first(send, side, present, slot=None):
+        @pl.when(present)
+        def _():
+            if slot is not None:
+                pl.semaphore_wait(hello.at[slot], 1)
+
+            @pl.loop(0, chunks)
+            def _(step):
+                send(0, side, step)
+
+    send_first(send_rows, 0, down_earlier)
+    send_first(send_rows, 1, up_earlier)
+    send_first(send_cols, 0, has_left)
 
     local = pltpu.make_async_copy(x_ref, buf0.at[:, 1 : rows + 1, 1 : cols + 1], in_sem.at[0])
     small = [
@@ -195,6 +217,13 @@
     for copy in small:
         copy.start()
     local.start()
+    send_first(send_rows, 1, up_later, 0)
+    send_first(send_cols, 1, has_right, 2)
+    send_first(send_rows, 0, down_later, 1)
+
+    @pl.when(t == 0)
+    def _():
+        pl.semaphore_wait(hello.at[3], 1)
 
     for buf in bufs:
         for row, present in ((0, has_down), (rows + 1, has_up)):
@@ -341,8 +370,9 @@
         for layer in range(2):
             e_copy(layer).wait_send()
 
-    lag = LEAD + 1
     for layer in range(2):
+        lag = LEADS[layer] + 1
+
         @pl.loop(0, chunks + lag)
         def _(step):
             @pl.when(step == lag)
@@ -440,6 +470,7 @@
             dma((2, 2, 2, chunks)), dma((2, 2, 2, chunks)),
             dma((2,)), dma((2,)),
             dma((4,)), dma((chunks,)),
+            pltpu.SemaphoreType.REGULAR((4,)),
         ],
         compiler_params=pltpu.CompilerParams(
             collective_id=0, has_side_effects=True, vmem_limit_bytes=40 * 1024 * 1024

time: 34.8 us -> 33.9 us (0.974)
  Pallas kernels: 33.7 us -> 32.8 us
    pallas_call x1, Pallas kernels: 33.7 us -> 32.8 us  [shards(): pl.pallas_call(functools.partial(kernel, sizes), out_shape=jax.ShapeDtype...]
where the time goes in v3:
time: 33.9 us; the launch traced here: 33.8 us
  Pallas kernels  32.8 us (97%)
  local copies, waits for them, and re-layouts  0.97 us (3%)
    pallas_call x1, Pallas kernels, shards(): pl.pallas_call(functools.partial(kernel, sizes), out_shape=jax.ShapeDtype...  32.8 us
    unnamed x1, local copies, waits for them, and re-layouts  0.97 us

profile of v3, /device:TPU:7, one launch (start us, length us, event | category | flops | bytes accessed | tf_op | source)
XLA Modules:
  0.0 33.8 jit_solution(17447652515112748411)
XLA Ops:
  0.0 32.8 %shard_map.46 = bf16[8,2,4,64,128]{4,3,2,1,0:T(8,128)(2,1)S(1)} custom-call(bf16[8,2,4,64,128]{4,3,2,1,0:T(8,128)(2,1)} %x_ref.1, bf16[128,9]{1,0:T(8,128)(2,1)} %bitcast.6, bf16[128,9]{1,0:T(8,128)(2,1)} %bitcast.7, f32[2,8]{1,0:T(2,128)} %bias_hbm.1), custom_call_target="tpu_custom_call" | custom-call | tf_op jit(solution)/shard_map/pallas_call | solution.py:449
  32.8 1.0 %copy.6 = bf16[8,2,4,64,128]{4,3,2,1,0:T(8,128)(2,1)} copy(bf16[8,2,4,64,128]{4,3,2,1,0:T(8,128)(2,1)S(1)} %shard_map.46) | data formatting | bytes 2097152

commit v4 on v3

--- a/solution.py
+++ b/solution.py
@@ -11,7 +11,11 @@
 BF16 = jnp.bfloat16
 F32 = jnp.float32
 STEP = 16
-LEADS = (3, 3)
+FAR, NEAR, INNER = 0, 1, 2
+ORDERS = (
+    ((FAR, 0), (NEAR, 0), (FAR, 1), (NEAR, 1), (FAR, 2), (NEAR, 2), (FAR, 3), (NEAR, 3), (INNER, 0), (INNER, 1), (INNER, 2), (INNER, 3)),
+    ((FAR, 0), (NEAR, 0), (FAR, 1), (NEAR, 1), (FAR, 2), (NEAR, 2), (FAR, 3), (NEAR, 3), (INNER, 0), (INNER, 1), (INNER, 2), (INNER, 3)),
+)
 Z_RING = 4
 PAD = 8
 
@@ -84,16 +88,23 @@
     def order(step):
         return (chunks - 1 - step) + t * (2 * step - (chunks - 1))
 
+    odd = lax.rem(s, 2)
+    part_cols = (
+        pl.ds(1 + (cols - 1) * odd, 1), pl.ds(cols - (cols - 1) * odd, 1), pl.ds(2, cols - 2),
+    )
+    part_cols_in = (
+        pl.ds((cols - 1) * odd, 1), pl.ds(cols - 1 - (cols - 1) * odd, 1), pl.ds(1, cols - 2),
+    )
+
     def z_copy(layer, side, part, block):
         ks = rows_of(block)
-        lo, hi = ((1, 2), (cols, cols + 1), (2, cols))[part]
         if layer == 0:
-            src = x_ref.at[:, 0 if side == 0 else rows - 1, lo - 1 : hi - 1, ks]
+            src = x_ref.at[:, 0 if side == 0 else rows - 1, part_cols_in[part], ks]
         else:
-            src = buf1.at[:, 1 if side == 0 else rows, lo:hi, ks]
+            src = buf1.at[:, 1 if side == 0 else rows, part_cols[part], ks]
         return pltpu.make_async_remote_copy(
             src_ref=src,
-            dst_ref=bufs[layer].at[:, rows + 1 if side == 0 else 0, lo:hi, ks],
+            dst_ref=bufs[layer].at[:, rows + 1 if side == 0 else 0, part_cols[part], ks],
             send_sem=z_send.at[layer, side, part, block],
             recv_sem=z_recv.at[layer, side, part, block],
             device_id=down if side == 0 else up,
@@ -115,15 +126,19 @@
             device_id_type=MESH,
         )
 
-    def c_copy(layer, side, end, block):
+    far_side = {"scol": lax.rem(s + n_col - 1 + 2 * odd, n_col)}
+    near_side = {"scol": lax.rem(s + n_col + 1 - 2 * odd, n_col)}
+
+    def c_copy(layer, part, end, block):
         ks = rows_of(block)
         row = 0 if end == 0 else rows + 1
+        to_right = odd if part == FAR else 1 - odd
         return pltpu.make_async_remote_copy(
-            src_ref=bufs[layer].at[:, row, 1 if side == 0 else cols, ks],
-            dst_ref=bufs[layer].at[:, row, cols + 1 if side == 0 else 0, ks],
-            send_sem=c_send.at[layer, side, end, block],
-            recv_sem=c_recv.at[layer, side, end, block],
-            device_id=left if side == 0 else right,
+            src_ref=bufs[layer].at[:, row, 1 + (cols - 1) * to_right, ks],
+            dst_ref=bufs[layer].at[:, row, (cols + 1) * (1 - to_right), ks],
+            send_sem=c_send.at[layer, part, end, block],
+            recv_sem=c_recv.at[layer, part, end, block],
+            device_id=far_side if part == FAR else near_side,
             device_id_type=MESH,
         )
 
@@ -140,6 +155,9 @@
     z_sides = ((0, has_down, has_up), (1, has_up, has_down))
     j_sides = ((0, has_left, has_right), (1, has_right, has_left))
     ends = ((0, has_down), (1, has_up))
+    has_far = (has_right & (odd == 1)) | (has_left & (odd == 0))
+    has_near = (has_right & (odd == 0)) | (has_left & (odd == 1))
+    beside = (has_far, has_near)
 
     first, last = lax.rem(r, Z_RING) == 0, lax.rem(r, Z_RING) == Z_RING - 1
     up_later, down_later = has_up & jnp.logical_not(last), has_down & first
@@ -165,44 +183,32 @@
         def _():
             pl.semaphore_signal(hello.at[slot], inc=1, device_id=device, device_id_type=MESH)
 
-    def send_rows(layer, side, step):
-        z_copy(layer, side, 0, order(step)).start()
-        z_copy(layer, side, 1, order(step)).start()
-
-        lead = LEADS[layer]
-
-        @pl.when(step >= lead)
-        def _():
-            z_copy(layer, side, 2, order(step - lead)).start()
-
-        @pl.when(step == chunks - 1)
-        def _():
-            for late in range(lead):
-                z_copy(layer, side, 2, order(chunks - lead + late)).start()
-
-    def send_cols(layer, side, step):
-        j_copy(layer, side, order(step)).start()
-
-    def send_chunk(layer, step):
+    def send_rows(layer, side, items):
+        for part, step in items:
+            z_copy(layer, side, part, order(step)).start()
+
+    def send_cols(layer, side, items):
+        for part, step in items:
+            if part == FAR:
+                j_copy(layer, side, order(step)).start()
+
+    def send_items(layer, items):
         for side, sends, _ in z_sides:
             @pl.when(sends)
             def _():
-                send_rows(layer, side, step)
+                send_rows(layer, side, items)
 
         for side, sends, _ in j_sides:
             @pl.when(sends)
             def _():
-                send_cols(layer, side, step)
+                send_cols(layer, side, items)
 
     def send_first(send, side, present, slot=None):
         @pl.when(present)
         def _():
             if slot is not None:
                 pl.semaphore_wait(hello.at[slot], 1)
-
-            @pl.loop(0, chunks)
-            def _(step):
-                send(0, side, step)
+            send(0, side, ORDERS[0])
 
     send_first(send_rows, 0, down_earlier)
     send_first(send_rows, 1, up_earlier)
@@ -362,72 +368,73 @@
                     def _():
                         j_copy(layer, side, block).wait_send()
 
+                for part in (FAR, NEAR):
                     for end, present in ends:
-                        @pl.when(sends & present)
+                        @pl.when(beside[part] & present)
                         def _():
-                            c_copy(layer, side, end, block).wait_send()
+                            c_copy(layer, part, end, block).wait_send()
 
         for layer in range(2):
             e_copy(layer).wait_send()
 
+    def take_outer(layer, part, step):
+        block = order(step)
+        for end, present in ends:
+            @pl.when(present)
+            def _():
+                z_copy(layer, 1 - end, part, block).wait_recv()
+
+                @pl.when(beside[part])
+                def _():
+                    c_copy(layer, part, end, block).start()
+
+    def take_cols(layer, step):
+        block = order(step)
+        for side, _, receives in j_sides:
+            @pl.when(receives)
+            def _():
+                j_copy(layer, side, block).wait_recv()
+
+        own_rows_pass(layer, block)
+
+    def take_inner(layer, step):
+        block = order(step)
+        for part in (FAR, NEAR):
+            for end, present in ends:
+                @pl.when(beside[part] & present)
+                def _():
+                    c_copy(layer, part, end, block).wait_recv()
+
+        for end, present in ends:
+            @pl.when(present)
+            def _():
+                z_copy(layer, 1 - end, INNER, block).wait_recv()
+
+        finish(layer, block)
+
+    unsent = list(ORDERS[1])
     for layer in range(2):
-        lag = LEADS[layer] + 1
-
-        @pl.loop(0, chunks + lag)
-        def _(step):
-            @pl.when(step == lag)
-            def _():
+        for part, step in ORDERS[layer]:
+            if part != INNER:
+                take_outer(layer, part, step)
+                if part == NEAR:
+                    take_cols(layer, step)
+                continue
+            if step == 0:
                 edge_add(layer)
-
+            if layer == 1 and step == chunks - 1:
+                wait_sends()
+            take_inner(layer, step)
             if layer == 1:
-                @pl.when(step == chunks + lag - 1)
-                def _():
-                    wait_sends()
-
-            @pl.when(step >= lag)
-            def _():
-                block = order(step - lag)
-                for side, _, receives in j_sides:
-                    for end, present in ends:
-                        @pl.when(receives & present)
-                        def _():
-                            c_copy(layer, side, end, block).wait_recv()
-
-                for end, present in ends:
-                    @pl.when(present)
-                    def _():
-                        z_copy(layer, 1 - end, 2, block).wait_recv()
-
-                finish(layer, block)
-                if layer == 0:
-                    send_chunk(1, step - lag)
-                    target_pass(1, block)
-
-                    @pl.when(step == lag)
-                    def _():
-                        edge_start(1)
-                else:
-                    out_copy(block).start()
-
-            @pl.when(step < chunks)
-            def _():
-                block = order(step)
-                for end, present in ends:
-                    @pl.when(present)
-                    def _():
-                        z_copy(layer, 1 - end, 0, block).wait_recv()
-                        z_copy(layer, 1 - end, 1, block).wait_recv()
-                        for side, sends, _ in j_sides:
-                            @pl.when(sends)
-                            def _():
-                                c_copy(layer, side, end, block).start()
-
-                for side, _, receives in j_sides:
-                    @pl.when(receives)
-                    def _():
-                        j_copy(layer, side, block).wait_recv()
-
-                own_rows_pass(layer, block)
+                out_copy(order(step)).start()
+                continue
+            ready = []
+            while unsent and unsent[0][1] <= step:
+                ready.append(unsent.pop(0))
+            send_items(1, ready)
+            target_pass(1, order(step))
+            if step == 0:
+                edge_start(1)
 
     @pl.loop(0, chunks)
     def _(block):

time: 33.9 us -> 33.3 us (0.982)
  Pallas kernels: 32.8 us -> 32.2 us
    pallas_call x1, Pallas kernels: 32.8 us -> 32.2 us  [shards(): pl.pallas_call(functools.partial(kernel, sizes), out_shape=jax.ShapeDtype...]
where the time goes in v4:
time: 33.3 us; the launch traced here: 33.2 us
  Pallas kernels  32.2 us (97%)
  local copies, waits for them, and re-layouts  0.97 us (3%)
    pallas_call x1, Pallas kernels, shards(): pl.pallas_call(functools.partial(kernel, sizes), out_shape=jax.ShapeDtype...  32.2 us
    unnamed x1, local copies, waits for them, and re-layouts  0.97 us

profile of v4, /device:TPU:7, one launch (start us, length us, event | category | flops | bytes accessed | tf_op | source)
XLA Modules:
  0.0 33.2 jit_solution(13990384043207462391)
XLA Ops:
  0.0 32.2 %shard_map.46 = bf16[8,2,4,64,128]{4,3,2,1,0:T(8,128)(2,1)S(1)} custom-call(bf16[8,2,4,64,128]{4,3,2,1,0:T(8,128)(2,1)} %x_ref.1, bf16[128,9]{1,0:T(8,128)(2,1)} %bitcast.6, bf16[128,9]{1,0:T(8,128)(2,1)} %bitcast.7, f32[2,8]{1,0:T(2,128)} %bias_hbm.1), custom_call_target="tpu_custom_call" | custom-call | tf_op jit(solution)/shard_map/pallas_call | solution.py:456
  32.2 1.0 %copy.6 = bf16[8,2,4,64,128]{4,3,2,1,0:T(8,128)(2,1)} copy(bf16[8,2,4,64,128]{4,3,2,1,0:T(8,128)(2,1)S(1)} %shard_map.46) | data formatting | bytes 2097152

commit v5 on v4

--- a/solution.py
+++ b/solution.py
@@ -68,8 +68,8 @@
 def kernel(
     sizes, x_ref, ws_hbm, wt_hbm, bias_hbm, out_ref,
     ws_ref, wt_ref, bias_ref,
-    buf0, buf1, sums0, sums1, src_mat, tgt_mat, edge_out, edge_in, staged,
-    z_send, z_recv, j_send, j_recv, c_send, c_recv, e_send, e_recv, in_sem, out_sem, hello,
+    buf0, buf1, sums0, sums1, src_mat, tgt_mat, edge_out, edge_in,
+    z_send, z_recv, j_send, j_recv, c_send, c_recv, e_send, e_recv, in_sem, hello,
 ):
     n_row, n_col = sizes
     channels, rows, cols, depth, width = x_ref.shape
@@ -224,8 +224,8 @@
         copy.start()
     local.start()
     send_first(send_rows, 1, up_later, 0)
+    send_first(send_rows, 0, down_later, 1)
     send_first(send_cols, 1, has_right, 2)
-    send_first(send_rows, 0, down_later, 1)
 
     @pl.when(t == 0)
     def _():
@@ -335,13 +335,7 @@
                     if layer == 0:
                         buf1[:, i + 1, j + 1, ks] = value
                     else:
-                        staged[:, i, j, ks] = value
-
-    def out_copy(block):
-        ks = rows_of(block)
-        return pltpu.make_async_copy(
-            staged.at[:, :, :, ks], out_ref.at[:, :, :, ks], out_sem.at[block]
-        )
+                        out_ref[:, i, j, ks] = value
 
     local.wait()
 
@@ -426,7 +420,6 @@
                 wait_sends()
             take_inner(layer, step)
             if layer == 1:
-                out_copy(order(step)).start()
                 continue
             ready = []
             while unsent and unsent[0][1] <= step:
@@ -435,10 +428,6 @@
             target_pass(1, order(step))
             if step == 0:
                 edge_start(1)
-
-    @pl.loop(0, chunks)
-    def _(block):
-        out_copy(block).wait()
 
 
 def by_channels(weight):
@@ -462,7 +451,7 @@
             pl.BlockSpec(memory_space=pltpu.HBM),
             pl.BlockSpec(memory_space=pltpu.HBM),
         ],
-        out_specs=pl.BlockSpec(memory_space=pl.ANY),
+        out_specs=pl.BlockSpec(memory_space=pltpu.VMEM),
         scratch_shapes=[
             pltpu.VMEM((2 * channels * channels, 9), BF16),
             pltpu.VMEM((2 * channels * channels, 9), BF16),
@@ -471,12 +460,11 @@
             pltpu.VMEM((2, 256, 12 * 128), BF16),
             pltpu.VMEM((2, 256, 3 * 128), BF16),
             edges, edges,
-            pltpu.VMEM(volume.shape, BF16),
             dma((2, 2, 3, chunks)), dma((2, 2, 3, chunks)),
             dma((2, 2, chunks)), dma((2, 2, chunks)),
             dma((2, 2, 2, chunks)), dma((2, 2, 2, chunks)),
             dma((2,)), dma((2,)),
-            dma((4,)), dma((chunks,)),
+            dma((4,)),
             pltpu.SemaphoreType.REGULAR((4,)),
         ],
         compiler_params=pltpu.CompilerParams(

time: 33.3 us -> 33.2 us (level)
  no operation moved by 1% of the time
where the time goes in v5:
time: 33.2 us; the launch traced here: 33.1 us
  Pallas kernels  32.1 us (97%)
  local copies, waits for them, and re-layouts  0.97 us (3%)
    pallas_call x1, Pallas kernels, shards(): pl.pallas_call(functools.partial(kernel, sizes), out_shape=jax.ShapeDtype...  32.1 us
    unnamed x1, local copies, waits for them, and re-layouts  0.97 us

profile of v5, /device:TPU:7, one launch (start us, length us, event | category | flops | bytes accessed | tf_op | source)
XLA Modules:
  0.0 33.1 jit_solution(15026223172522836096)
XLA Ops:
  0.0 32.1 %shard_map.46 = bf16[8,2,4,64,128]{4,3,2,1,0:T(8,128)(2,1)S(1)} custom-call(bf16[8,2,4,64,128]{4,3,2,1,0:T(8,128)(2,1)} %x_ref.1, bf16[128,9]{1,0:T(8,128)(2,1)} %bitcast.6, bf16[128,9]{1,0:T(8,128)(2,1)} %bitcast.7, f32[2,8]{1,0:T(2,128)} %bias_hbm.1), custom_call_target="tpu_custom_call" | custom-call | tf_op jit(solution)/shard_map/pallas_call | solution.py:445
  32.1 1.0 %copy.6 = bf16[8,2,4,64,128]{4,3,2,1,0:T(8,128)(2,1)} copy(bf16[8,2,4,64,128]{4,3,2,1,0:T(8,128)(2,1)S(1)} %shard_map.46) | data formatting | bytes 2097152
